TPU v7x, 32 devices: a whole 2x2x4 slice. The times are simulated.
32 devices in a mesh: col: 8 (over z, x), row: 4 (over y, core).
Axes of the slice: x: 2, y: 2, z: 4, core: 2. Of those that a mesh axis runs over, the one named last changes fastest.
Arguments:
- positions: float32 [3, 131072], P(None, ('col', 'row')), may hold values from -6 to 6
- velocities: float32 [3, 131072], P(None, ('col', 'row')), may hold values from -4 to 4
- masses: float32 [131072], P(('col', 'row')), may hold values from 7.629395e-09 to 7.6293945e-05
- active_index: int32 [2048], P(('col', 'row')), may hold values from 0 to 4095, as said below
- active_count: int32 [32], P(('col', 'row')), may hold values from 1 to 64, as said below
Outputs:
- accel: float32 [3, 2048], P(None, ('col', 'row'))
- jerk: float32 [3, 2048], P(None, ('col', 'row'))
Inputs may be any that keep to these rules, and one draw needn't show every extreme that they name: `active_index`: entries of block b (slots b * 64 to (b + 1) * 64 - 1) index stars of the block of 4096 that block b owns; the entries of one block are distinct. `active_count`: number of used slots of each block, counted from the block's first slot. Some block uses all 64 slots in every draw.
All inputs are finite; a program needn't handle non-finite values.
Results may differ from a plain program's by a relative error of at most 0.0003.
Values sent between devices are 32-bit elements; how exact they have to be, the bound alone decides.
No kernel may reach another device: no remote copies, remote signals or barrier semaphores. Data moves between devices by JAX's collectives and lax.ppermute only.
A program may use at most 64 MiB of HBM per device.

v0:
```python
import math

import jax
import jax.numpy as jnp
from jax import lax
from jax.sharding import PartitionSpec as P

SOFTEN = 0.0001


def pair_block(actives, field_piece):
    offset = field_piece[0:3, None, :] - actives[0:3, :, None]
    rel_vel = field_piece[3:6, None, :] - actives[3:6, :, None]
    squared = jnp.sum(offset * offset, axis=0) + SOFTEN
    inverse = 1.0 / squared
    strength = field_piece[6][None, :] * inverse / jnp.sqrt(squared)
    radial = 3.0 * jnp.sum(offset * rel_vel, axis=0) * inverse
    accel_part = jnp.sum(strength[None] * offset, axis=2)
    jerk_part = jnp.sum(strength[None] * (rel_vel - radial[None] * offset), axis=2)
    return jnp.concatenate([accel_part, jerk_part], axis=0)


def pair_terms(actives, field_stars):
    width_all = field_stars.shape[1]
    block_cols = math.gcd(width_all, 512)
    count_blocks = width_all // block_cols
    pieces = field_stars.reshape(7, count_blocks, block_cols).transpose(1, 0, 2)
    active_width = actives.shape[1]
    active_block = math.gcd(active_width, 1024)
    active_groups = active_width // active_block
    grouped = actives.reshape(6, active_groups, active_block).transpose(1, 0, 2)

    def one_group(group_actives):

        def add_piece(summed, field_piece):
            return (summed + pair_block(group_actives, field_piece), None)

        summed, unused = lax.scan(add_piece, jnp.zeros((6, active_block), jnp.float32), pieces)
        return summed

    results = lax.map(one_group, grouped)
    return results.transpose(1, 0, 2).reshape(6, active_width)


def body(positions, velocities, masses, active_index, active_count):
    slots = active_index.shape[0]
    own_actives = jnp.concatenate(
        [jnp.take(positions, active_index, axis=1), jnp.take(velocities, active_index, axis=1)],
        axis=0,
    )
    field_stars = jnp.concatenate([positions, velocities, masses[None, :]], axis=0)
    used_slot = jnp.arange(slots, dtype=jnp.int32) < active_count[0]
    all_actives = lax.all_gather(own_actives, ("col", "row"), axis=1, tiled=True)
    partial_value = pair_terms(all_actives, field_stars)
    own_terms = lax.psum_scatter(partial_value, ("col", "row"), scatter_dimension=1, tiled=True)
    own_terms = jnp.where(used_slot[None, :], own_terms, 0.0)
    return (own_terms[0:3], own_terms[3:6])


def solution(mesh):
    return jax.shard_map(
        body,
        mesh=mesh,
        in_specs=(
            P(None, ("col", "row")),
            P(None, ("col", "row")),
            P(("col", "row")),
            P(("col", "row")),
            P(("col", "row")),
        ),
        out_specs=(P(None, ("col", "row")), P(None, ("col", "row"))),
        check_vma=False,
    )
```

profile of v0, /device:TPU:0, one launch (start us, length us, event | category | flops | bytes accessed | tf_op | source)
XLA Modules:
  0.0 327.3 jit_solution(7568245778453511347)
XLA Ops:
  7.2 0.7 compare_select_fusion
  7.9 0.7 compare_and_fusion
  8.6 2.9 copy.28
  11.5 0.6 copy.29
  12.1 2.2 gather_fusion
  14.3 0.6 gather_fusion.1
  14.9 0.1 select_bitcast_fusion.1
  15.1 43.6 %all-gather = f32[32,64,6]{1,2,0:T(8,128)S(1)} all-gather(f32[1,64,6]{1,2,0:T(8,128)S(1)} %maximum_bitcast_fusion.1), channel_id=1, replica_groups=mesh['col'=8,'row'=4] {'col','row'}, dimensions={0}, use_global_device_ids=true | all-gather | bytes 50688 | tf_op jit(solution)/shard_map/all_gather | solution.py:53
  58.7 0.1 reshape.85
  59.0 127.6 %while.22 = (s32[]{:T(128)}, f32[2,6,1024]{2,1,0:T(8,128)S(1)}, f32[2,6,1024]{2,0,1:T(2,128)S(1)}, f32[8,7,512]{2,1,0:T(8,128)S(1)}, s32[]{:T(128)}, /*index=5*/s32[]{:T(128)}, s32[]{:T(128)}, s32[]{:T(128)}, s32[]{}, s32[]{}) while((s32[]{:T(128)}, f32[2,6,1024]{2,1,0:T(8,128)S(1)}, f32[2,6,1024]{2,0,1:T(2,128)S(1)}, ...), condition=%wide.region_7.9_spmd, body=%wide.region_0.8_spmd.sunk | while | flops 24129540 | bytes 17193272 | solution.py:41
  59.0 63.7 %while.23 = (s32[]{:T(128)}, f32[6,1024]{1,0:T(8,128)S(1)}, f32[8,7,512]{2,1,0:T(8,128)S(1)}, f32[6,1024]{1,0:T(8,128)S(1)}, s32[]{:T(128)}, /*index=5*/s32[]{:T(128)}, s32[]{}, s32[]{}) while((s32[]{:T(128)}, f32[6,1024]{1,0:T(8,128)S(1)}, f32[8,7,512]{2,1,0:T(8,128)S(1)}, f32[6,1024]{1,0:T(8,128)S(1)}, s32[]{:T(128)}, ...), condition=%wide.region_6.7_spmd.clone, body=%wide.region_1.6_spmd.clone.sunk | while | flops 24129540 | bytes 17029252 | solution.py:38
  59.1 3.1 fusion.11
  62.2 2.2 multiply_multiply_fusion.2
  64.4 2.6 fusion.12
  67.0 3.1 fusion.11
  70.2 2.2 multiply_multiply_fusion.2
  72.3 2.6 fusion.12
  75.0 3.1 fusion.11
  78.1 2.2 multiply_multiply_fusion.2
  80.3 2.6 fusion.12
  83.0 3.1 fusion.11
  86.1 2.2 multiply_multiply_fusion.2
  88.2 2.6 fusion.12
  90.9 3.1 fusion.11
  94.0 2.2 multiply_multiply_fusion.2
  96.2 2.6 fusion.12
  98.9 3.1 fusion.11
  102.0 2.2 multiply_multiply_fusion.2
  104.2 2.6 fusion.12
  106.9 3.1 fusion.11
  110.0 2.2 multiply_multiply_fusion.2
  112.1 2.6 fusion.12
  114.8 3.1 fusion.11
  117.9 2.2 multiply_multiply_fusion.2
  120.1 2.6 fusion.12
  122.8 63.7 %while.23 = (s32[]{:T(128)}, f32[6,1024]{1,0:T(8,128)S(1)}, f32[8,7,512]{2,1,0:T(8,128)S(1)}, f32[6,1024]{1,0:T(8,128)S(1)}, s32[]{:T(128)}, /*index=5*/s32[]{:T(128)}, s32[]{}, s32[]{}) while((s32[]{:T(128)}, f32[6,1024]{1,0:T(8,128)S(1)}, f32[8,7,512]{2,1,0:T(8,128)S(1)}, f32[6,1024]{1,0:T(8,128)S(1)}, s32[]{:T(128)}, ...), condition=%wide.region_6.7_spmd.clone, body=%wide.region_1.6_spmd.clone.sunk | while | flops 24129540 | bytes 17029252 | solution.py:38
  122.9 3.1 fusion.11
  126.0 2.2 multiply_multiply_fusion.2
  128.2 2.6 fusion.12
  130.9 3.1 fusion.11
  134.0 2.2 multiply_multiply_fusion.2
  136.1 2.6 fusion.12
  138.8 3.1 fusion.11
  141.9 2.2 multiply_multiply_fusion.2
  144.1 2.6 fusion.12
  146.8 3.1 fusion.11
  149.9 2.2 multiply_multiply_fusion.2
  152.1 2.6 fusion.12
  154.7 3.1 fusion.11
  157.9 2.2 multiply_multiply_fusion.2
  160.0 2.6 fusion.12
  162.7 3.1 fusion.11
  165.8 2.2 multiply_multiply_fusion.2
  168.0 2.6 fusion.12
  170.7 3.1 fusion.11
  173.8 2.2 multiply_multiply_fusion.2
  175.9 2.6 fusion.12
  178.6 3.1 fusion.11
  181.7 2.2 multiply_multiply_fusion.2
  183.9 2.6 fusion.12
  186.6 1.4 copy.35
  188.6 130.4 %reduce-scatter.4.cloned.1.call-done = f32[64,6]{1,0:T(8,128)} async-done(((f32[2048,6]{1,0:T(8,128)}), f32[64,6]{1,0:T(8,128)}) %reduce-scatter.4.cloned.1.call-update) | async-done | bytes 1552
  319.0 0.8 copy.36
  319.8 0.6 fusion.6
  (90 shorter events, 1.1 us)
Async XLA Ops:
  7.2 4.3 %copy-start.1 = (f32[3,4096]{1,0:T(4,128)S(1)}, f32[3,4096]{1,0:T(4,128)}, u32[]{:S(2)}) copy-start(f32[3,4096]{1,0:T(4,128)} %param.12) | copy-start | bytes 147460
  7.2 311.8 %reduce-scatter.4.cloned.1.call-start = ((), (), s32[]{:S(2)}) async-start(), calls=%async_computation.1 | async-start | bytes 1081344
  8.5 50.3 %copy-start = (f32[3,4096]{1,0:T(4,128)S(1)}, f32[3,4096]{1,0:T(4,128)}, u32[]{:S(2)}) copy-start(f32[3,4096]{1,0:T(4,128)} %param.11) | copy-start | bytes 147460
  8.6 50.3 %copy-start.2 = (f32[4096]{0:T(1024)S(1)}, f32[4096]{0:T(1024)}, u32[]{:S(2)}) copy-start(f32[4096]{0:T(1024)} %param.13) | copy-start | bytes 49156
Sparse Core Ops, SparseCore 0:
  188.1 130.8 reduce-scatter.3
where the time goes:
time: 328 us; the launch traced here: 327 us
  waiting for transfers between devices  130 us (40%)
  other arithmetic  128 us (39%)
  blocking collectives  43.6 us (13%)
  between operations  14.8 us (5%)
  local copies, waits for them, and re-layouts  9.91 us (3%)
    unnamed x2, waiting for transfers between devices  130 us
    reduce_sum x16, other arithmetic, pair_block(): squared = jnp.sum(offset * offset, axis=0) + SOFTEN  49.7 us
    all_gather x1, blocking collectives, body(): lax.all_gather(own_actives, ('col', 'row'), axis=1, tiled=True)  43.6 us
    reduce_sum x16, other arithmetic, pair_block(): accel_part = jnp.sum(strength[None] * offset, axis=2)  41.7 us
    mul x16, other arithmetic, pair_block(): radial = 3.0 * jnp.sum(offset * rel_vel, axis=0) * inverse  34.4 us
  transfers between devices with their start and end apart: 1, of which 1 were waited for; matrix products, arithmetic and copies ran while one was open for 0% of the time, Pallas kernels for 0%

commit v1 on v0

v1 whole, which is shorter than its diff:
```python
import functools

import jax
import jax.numpy as jnp
import numpy as np
from jax import lax
from jax.experimental import pallas as pl
from jax.experimental.pallas import tpu as pltpu
from jax.sharding import PartitionSpec as P

AXES = ("col", "row")
SOFTEN = 0.0001
F32 = jnp.float32
CH = 16
GROUP = 16


def vmem():
    return pl.BlockSpec(memory_space=pltpu.VMEM)


def smem():
    return pl.BlockSpec(memory_space=pltpu.SMEM)


def prepare_kernel(parts, index_ref, count_ref, pos_ref, vel_ref, mass_ref, send_ref, stars_ref):
    slots = index_ref.shape[0]
    stars_ref[0:3, :] = pos_ref[...]
    stars_ref[3:6, :] = vel_ref[...]
    stars_ref[6:7, :] = mass_ref[...]
    stars_ref[7:8, :] = jnp.zeros_like(mass_ref)
    lane = lax.broadcasted_iota(jnp.int32, (8, 128), 1)
    row = lax.broadcasted_iota(jnp.int32, (8, 128), 0)
    picked = jnp.zeros((8, 128), F32)
    for slot in range(slots):
        star = index_ref[slot]
        tile = stars_ref[:, pl.ds(pl.multiple_of((star // 128) * 128, 128), 128)]
        moved = pltpu.roll(tile, (slot - star % 128) % 128, 1)
        picked = jnp.where(lane == slot, moved, picked)
    picked = jnp.where(row == 6, count_ref[0].astype(F32), picked)[:, :slots]

    def fill(part, carry):
        send_ref[part] = picked
        return carry

    lax.fori_loop(0, parts, fill, 0, unroll=8)


def pair_kernel(recv_ref, stars_ref, send_ref, count_smem, offset_smem, act_ref, sum_ref, acc_ref, sem):
    parts, _, slots = recv_ref.shape
    width = stars_ref.shape[1]
    copy = pltpu.make_async_copy(recv_ref.at[:, 6], count_smem, sem)
    copy.start()
    copy.wait()

    def offsets(part, total):
        offset_smem[part] = total
        used = count_smem[part, 0].astype(jnp.int32)
        return total + ((used + 7) // 8) * 8

    total = lax.fori_loop(0, parts, offsets, 0)

    def unpack(group, carry):
        turned = recv_ref[pl.ds(group * GROUP, GROUP)].reshape(GROUP * 8, slots).T
        for k in range(GROUP):
            first = pl.multiple_of(offset_smem[group * GROUP + k], 8)
            act_ref[pl.ds(first, slots), :] = pltpu.roll(turned, (128 - 8 * k) % 128, 1)
        return carry

    lax.fori_loop(0, parts // GROUP, unpack, 0)

    lane = lax.broadcasted_iota(jnp.int32, (CH, 128), 1)

    def collect(chunk):
        rows = pl.ds(pl.multiple_of(chunk * CH, CH), CH)
        sums = jnp.zeros((CH, 128), F32)
        for k in range(6):
            sums = jnp.where(lane == k, jnp.sum(acc_ref[k], axis=1, keepdims=True), sums)
        sum_ref[rows, :] = sums

    def chunk_step(chunk, carry):
        rows = pl.ds(pl.multiple_of(chunk * CH, CH), CH)
        collect(jnp.maximum(chunk - 1, 0))
        own = act_ref[rows, :]
        act = [jnp.broadcast_to(own[:, k : k + 1], (CH, 128)) for k in range(6)]
        acc = [jnp.zeros((CH, 128), F32) for _ in range(9)]
        for j in range(width // 128):
            star = [
                jnp.broadcast_to(stars_ref[k : k + 1, j * 128 : (j + 1) * 128], (CH, 128))
                for k in range(7)
            ]
            dx = [star[k] - act[k] for k in range(3)]
            dv = [star[3 + k] - act[3 + k] for k in range(3)]
            squared = dx[2] * dx[2] + (dx[1] * dx[1] + (dx[0] * dx[0] + SOFTEN))
            root = lax.rsqrt(squared)
            inverse = root * root
            strength = (star[6] * root) * inverse
            dot = dx[0] * dv[0] + dx[1] * dv[1] + dx[2] * dv[2]
            pull = (dot * inverse) * strength
            for k in range(3):
                acc[k] += strength * dx[k]
                acc[3 + k] += strength * dv[k]
                acc[6 + k] += pull * dx[k]
        for k in range(3):
            acc_ref[k] = acc[k]
            acc_ref[3 + k] = acc[3 + k] - 3.0 * acc[6 + k]
        return carry

    chunks = (total + CH - 1) // CH
    lax.fori_loop(0, chunks, chunk_step, 0)
    collect(chunks - 1)

    lane_all = lax.broadcasted_iota(jnp.int32, (slots, 128), 1)

    def pack(group, carry):
        turned = jnp.zeros((slots, 128), F32)
        for k in range(GROUP):
            first = pl.multiple_of(offset_smem[group * GROUP + k], 8)
            moved = pltpu.roll(sum_ref[pl.ds(first, slots), :], 8 * k, 1)
            turned = jnp.where((lane_all >= 8 * k) & (lane_all < 8 * k + 8), moved, turned)
        send_ref[pl.ds(group * GROUP, GROUP)] = turned.T.reshape(GROUP, 8, slots)
        return carry

    lax.fori_loop(0, parts // GROUP, pack, 0)


def finish_kernel(count_ref, recv_ref, accel_ref, jerk_ref):
    parts, _, slots = recv_ref.shape

    def add(part, total):
        return total + recv_ref[part]

    total = lax.fori_loop(1, parts, add, recv_ref[0], unroll=8)
    slot = lax.broadcasted_iota(jnp.int32, (8, slots), 1)
    total = jnp.where(slot < count_ref[0], total, 0.0)
    accel_ref[...] = total[0:3]
    jerk_ref[...] = total[3:6]


def body(parts, positions, velocities, masses, active_index, active_count):
    slots = active_index.shape[0]
    width = positions.shape[1]
    send, stars = pl.pallas_call(
        functools.partial(prepare_kernel, parts),
        out_shape=(
            jax.ShapeDtypeStruct((parts, 8, slots), F32),
            jax.ShapeDtypeStruct((8, width), F32),
        ),
        in_specs=[smem(), smem(), vmem(), vmem(), vmem()],
        out_specs=(vmem(), vmem()),
    )(active_index, active_count, positions, velocities, masses.reshape(1, width))
    received = lax.all_to_all(send, AXES, 0, 0)
    rows = parts * slots + slots
    partial_sums = pl.pallas_call(
        pair_kernel,
        out_shape=jax.ShapeDtypeStruct((parts, 8, slots), F32),
        in_specs=[vmem(), vmem()],
        out_specs=vmem(),
        scratch_shapes=[
            pltpu.SMEM((parts, slots), F32),
            pltpu.SMEM((parts,), jnp.int32),
            pltpu.VMEM((rows, 128), F32),
            pltpu.VMEM((rows, 128), F32),
            pltpu.VMEM((6, CH, 128), F32),
            pltpu.SemaphoreType.DMA,
        ],
        compiler_params=pltpu.CompilerParams(vmem_limit_bytes=48 * 1024 * 1024),
    )(received, stars)
    returned = lax.all_to_all(partial_sums, AXES, 0, 0)
    return pl.pallas_call(
        finish_kernel,
        out_shape=(
            jax.ShapeDtypeStruct((3, slots), F32),
            jax.ShapeDtypeStruct((3, slots), F32),
        ),
        in_specs=[smem(), vmem()],
        out_specs=(vmem(), vmem()),
    )(active_count, returned)


def solution(mesh):
    parts = int(np.prod([mesh.shape[axis] for axis in AXES]))
    return jax.shard_map(
        functools.partial(body, parts),
        mesh=mesh,
        in_specs=(P(None, AXES), P(None, AXES), P(AXES), P(AXES), P(AXES)),
        out_specs=(P(None, AXES), P(None, AXES)),
        check_vma=False,
    )
```

time: 328 us -> 61.9 us (0.19)
  waiting for transfers between devices: 130 us -> 0 us
  other arithmetic: 128 us -> 1.6 us
  Pallas kernels: 0 us -> 31.8 us
  blocking collectives: 43.6 us -> 23.6 us
  between operations: 14.8 us -> 1.33 us
  local copies, waits for them, and re-layouts: 9.91 us -> 3.28 us
    unnamed x2 -> x0, waiting for transfers between devices: 130 us -> none
    reduce_sum x32 -> x0, other arithmetic: 91.4 us -> none  [the longest x16 49.7 us: pair_block(): squared = jnp.sum(offset * offset, axis=0) + SOFTEN]
    all_gather x1 -> x0, blocking collectives: 43.6 us -> none  [body(): lax.all_gather(own_actives, ('col', 'row'), axis=1, tiled=True)]
    mul x16 -> x0, other arithmetic: 34.4 us -> none  [pair_block(): radial = 3.0 * jnp.sum(offset * rel_vel, axis=0) * inverse]
    pallas_call x0 -> x3, Pallas kernels: none -> 31.8 us  [the longest x1 28 us: body(): pl.pallas_call(pair_kernel, out_shape=jax.ShapeDtypeStruct((parts, 8, slo...]
    all_to_all x0 -> x2, blocking collectives: none -> 23.6 us  [the longest x1 14.5 us: body(): received = lax.all_to_all(send, AXES, 0, 0)]
  transfers between devices with their start and end apart: 1 -> 0, of which waited for: 1 -> 0; matrix products, arithmetic and copies ran while one was open for 0% -> 0% of each run, Pallas kernels for 0% -> 0%
where the time goes in v1:
time: 61.9 us; the launch traced here: 61.6 us
  Pallas kernels  31.8 us (51%)
  blocking collectives  23.6 us (38%)
  local copies, waits for them, and re-layouts  3.28 us (5%)
  other arithmetic  1.6 us (3%)
  between operations  1.33 us (2%)
    pallas_call x1, Pallas kernels, body(): pl.pallas_call(pair_kernel, out_shape=jax.ShapeDtypeStruct((parts, 8, slo...  28 us
    all_to_all x1, blocking collectives, body(): received = lax.all_to_all(send, AXES, 0, 0)  14.5 us
    all_to_all x1, blocking collectives, body(): returned = lax.all_to_all(partial_sums, AXES, 0, 0)  9.1 us
    unnamed x6, local copies, waits for them, and re-layouts  2.77 us
    pallas_call x1, Pallas kernels, body(): pl.pallas_call(functools.partial(prepare_kernel, parts), out_shape=(jax.S...  2.27 us
    pallas_call x1, Pallas kernels, body(): pl.pallas_call(finish_kernel, out_shape=(jax.ShapeDtypeStruct((3, slots),...  1.55 us

profile of v1, /device:TPU:0, one launch (start us, length us, event | category | flops | bytes accessed | tf_op | source)
XLA Modules:
  0.0 61.6 jit_solution(4698029710459350070)
XLA Ops:
  1.3 2.3 %shard_map.68 = (f32[32,8,64]{2,1,0:T(8,128)}, f32[8,4096]{1,0:T(8,128)}) custom-call(s32[64]{0:T(128)} %index_ref.1, s32[1]{0:T(128)S(6)} %copy.7.count_ref, f32[3,4096]{1,0:T(4,128)} %pos_ref.1, f32[3,4096]{1,0:T(4,128)} %vel_ref.1, f32[1,4096]{1,0:T(1,128)} %bitcast.1), custom_call_target="tpu_custom_call" | custom-call | tf_op jit(solution)/shard_map/pallas_call | solution.py:143
  3.5 1.0 %reshape.8 = f32[32,1,512]{2,1,0:T(1,128)S(1)} reshape(f32[32,8,64]{2,1,0:T(8,128)} %get-tuple-element.4) | data formatting | bytes 131072
  4.6 14.5 %all_to_all.10 = f32[32,1,512]{2,1,0:T(1,128)S(1)} all-to-all(f32[32,1,512]{2,1,0:T(1,128)S(1)} %reshape.8), channel_id=1, replica_groups=mesh['col'=8,'row'=4] {'col','row'}, dimensions={0} | all-to-all | bytes 131072 | tf_op jit(solution)/shard_map/all_to_all | solution.py:152
  19.1 0.5 broadcast
  19.6 0.8 %reduce = f32[32,512]{1,0:T(8,128)S(1)} reduce(f32[32,1,512]{2,1,0:T(1,128)S(1)} %all_to_all.10, f32[]{:T(128)} %broadcast), dimensions={1}, to_apply=%all_to_all.6.reduce_sub_computation | reduce | bytes 131076 | tf_op jit(solution)/shard_map/all_to_all | solution.py:152
  20.4 0.0 copy-start
  20.4 0.1 reshape.9.recv_ref
  20.5 0.8 %copy-done = f32[8,4096]{1,0:T(8,128)S(1)} copy-done((f32[8,4096]{1,0:T(8,128)S(1)}, f32[8,4096]{1,0:T(8,128)}, u32[]{:S(2)}) %copy-start) | copy-done | bytes 131096
  21.3 28.0 %shard_map.69 = f32[32,8,64]{2,1,0:T(8,128)S(1)} custom-call(f32[32,8,64]{2,1,0:T(8,128)S(1)} %reshape.9.recv_ref, f32[8,4096]{1,0:T(8,128)S(1)} %copy-done), custom_call_target="tpu_custom_call" | custom-call | tf_op jit(solution)/shard_map/pallas_call | solution.py:154
  49.3 0.1 reshape.10
  49.5 9.1 %all_to_all.11 = f32[32,1,512]{2,1,0:T(1,128)S(1)} all-to-all(f32[32,1,512]{2,1,0:T(1,128)S(1)} %reshape.10), channel_id=1, replica_groups=mesh['col'=8,'row'=4] {'col','row'}, dimensions={0} | all-to-all | bytes 131072 | tf_op jit(solution)/shard_map/all_to_all | solution.py:169
  58.6 0.8 %reduce.1 = f32[32,512]{1,0:T(8,128)S(1)} reduce(f32[32,1,512]{2,1,0:T(1,128)S(1)} %all_to_all.11, f32[]{:T(128)} %broadcast), dimensions={1}, to_apply=%all_to_all.7.reduce_sub_computation | reduce | bytes 131076 | tf_op jit(solution)/shard_map/all_to_all | solution.py:169
  59.4 0.7 %reshape.11.recv_ref = f32[32,8,64]{2,1,0:T(8,128)} reshape(f32[32,512]{1,0:T(8,128)S(1)} %reduce.1) | data formatting | bytes 131072
  60.1 1.5 %shard_map.70 = (f32[3,64]{1,0:T(4,128)}, f32[3,64]{1,0:T(4,128)}) custom-call(s32[1]{0:T(128)S(6)} %copy.7.count_ref, f32[32,8,64]{2,1,0:T(8,128)} %reshape.11.recv_ref), custom_call_target="tpu_custom_call" | custom-call | tf_op jit(solution)/shard_map/pallas_call | solution.py:170
Async XLA Ops:
  20.4 0.9 %copy-start = (f32[8,4096]{1,0:T(8,128)S(1)}, f32[8,4096]{1,0:T(8,128)}, u32[]{:S(2)}) copy-start(f32[8,4096]{1,0:T(8,128)} %get-tuple-element.5.stars_ref) | copy-start | bytes 393220

commit v2 on v1

v2 whole, which is shorter than its diff:
```python
import functools

import jax
import jax.numpy as jnp
import numpy as np
from jax import lax
from jax.experimental import pallas as pl
from jax.experimental.pallas import tpu as pltpu
from jax.sharding import PartitionSpec as P

AXES = ("col", "row")
SOFTEN = 0.0001
F32 = jnp.float32
BF16 = jnp.bfloat16
TILE = 128
CH = 16
BLOCK = 256
UNROLL = 4
PAIRS = ((0, 0), (1, 0), (0, 1), (1, 1), (2, 0), (0, 2))
RAW = 8 * len(PAIRS)
NN = (((1,), (0,)), ((), ()))
NT = (((1,), (1,)), ((), ()))


def vmem():
    return pl.BlockSpec(memory_space=pltpu.VMEM)


def smem():
    return pl.BlockSpec(memory_space=pltpu.SMEM)


def pieces(value):
    first = value.astype(BF16).astype(F32)
    rest = value - first
    second = rest.astype(BF16).astype(F32)
    return first, second, (rest - second).astype(BF16).astype(F32)


def prepare_kernel(parts, index_ref, count_ref, pos_ref, vel_ref, mass_ref, send_ref, pos_out, dot_ref, sum_ref, stars_ref):
    slots = index_ref.shape[0]
    pos, vel, mass = pos_ref[...], vel_ref[...], mass_ref[...]
    width = pos.shape[1]
    ones = jnp.ones_like(mass)
    cross = jnp.sum(pos * vel, axis=0, keepdims=True)
    stars_ref[...] = jnp.concatenate([pos, vel, cross, ones], axis=0)
    pos_out[...] = jnp.concatenate([pos, jnp.zeros((5, width), F32)], axis=0)
    lane = lax.broadcasted_iota(jnp.int32, (8, 128), 1)
    picked = jnp.zeros((8, 128), F32)
    for slot in range(slots):
        star = index_ref[slot]
        tile = stars_ref[:, pl.ds(pl.multiple_of((star // 128) * 128, 128), 128)]
        moved = pltpu.roll(tile, (slot - star % 128) % 128, 1)
        picked = jnp.where(lane == slot, moved, picked)
    picked = jnp.where(lane < slots, picked, count_ref[0].astype(F32))

    def fill(part, carry):
        send_ref[part] = picked
        return carry

    lax.fori_loop(0, parts, fill, 0, unroll=8)
    heavy = 3.0 * mass
    dot_rows = jnp.concatenate([-heavy * vel, -heavy * pos, heavy, heavy * cross], axis=0)
    dots = [piece.astype(BF16) for piece in pieces(dot_rows)]
    for k, (mine, _) in enumerate(PAIRS):
        dot_ref[8 * k : 8 * k + 8, :] = dots[mine]
    dot_ref[RAW:, :] = jnp.zeros((128 - RAW, width), BF16)
    sum_rows = jnp.concatenate([mass * pos, mass * vel, mass, jnp.zeros_like(mass)], axis=0)
    for k, piece in enumerate(pieces(sum_rows)):
        sum_ref[8 * k : 8 * k + 8, :] = piece.astype(BF16)


def pair_kernel(slots, recv_ref, pos_ref, dot_ref, sum_ref, send_ref, count_smem, offset_smem, act_ref, own_ref, pull_ref, res_ref, sem):
    parts = recv_ref.shape[0]
    width = pos_ref.shape[1]
    copy = pltpu.make_async_copy(recv_ref.at[:, 0], count_smem, sem)
    copy.start()
    copy.wait()

    def offsets(part, total):
        offset_smem[part] = total
        used = count_smem[part, 127].astype(jnp.int32)
        return total + ((used + 7) // 8) * 8

    total = lax.fori_loop(0, parts, offsets, 0)

    def unpack(part, carry):
        own = recv_ref[part]
        split = pieces(own)
        rows = [split[theirs] for _, theirs in PAIRS] + [own]
        rows.append(jnp.zeros((128 - 8 * len(rows), 128), F32))
        first = pl.multiple_of(offset_smem[part], 8)
        act_ref[pl.ds(first, slots), :] = jnp.concatenate(rows, axis=0).T[:slots]
        return carry

    lax.fori_loop(0, parts, unpack, 0, unroll=4)

    def tile_step(tile, carry):
        rows = pl.ds(pl.multiple_of(tile * TILE, TILE), TILE)
        act = act_ref[rows, :]
        for k in range(3):
            own_ref[k] = jnp.broadcast_to(act[:, RAW + k : RAW + k + 1], (TILE, 128))
            pull_ref[k] = jnp.zeros((TILE, 128), F32)
        left = act.astype(BF16)

        def block_step(step, sums):
            for block in range(UNROLL):
                cols = pl.ds(pl.multiple_of((step * UNROLL + block) * BLOCK, BLOCK), BLOCK)
                dot = lax.dot_general(left, dot_ref[:, cols], NN, preferred_element_type=F32)
                high, low = [], []
                for chunk in range(TILE // CH):
                    part = slice(chunk * CH, chunk * CH + CH)
                    own = [own_ref[k, part, :] for k in range(3)]
                    acc = [pull_ref[k, part, :] for k in range(3)]
                    highs, lows = [], []
                    for half in range(BLOCK // 128):
                        lanes = pl.ds(pl.multiple_of((step * UNROLL + block) * BLOCK + half * 128, 128), 128)
                        star = [jnp.broadcast_to(pos_ref[k : k + 1, lanes], (CH, 128)) for k in range(3)]
                        dx = [star[k] - own[k] for k in range(3)]
                        squared = dx[2] * dx[2] + (dx[1] * dx[1] + (dx[0] * dx[0] + SOFTEN))
                        root = lax.rsqrt(squared)
                        inverse = root * root
                        cube = root * inverse
                        pull = (dot[part, half * 128 : half * 128 + 128] * inverse) * cube
                        for k in range(3):
                            acc[k] += pull * dx[k]
                        first = cube.astype(BF16)
                        highs.append(first)
                        lows.append((cube - first.astype(F32)).astype(BF16))
                    for k in range(3):
                        pull_ref[k, part, :] = acc[k]
                    high.append(jnp.concatenate(highs, axis=1))
                    low.append(jnp.concatenate(lows, axis=1))
                field = sum_ref[:, cols]
                sums += lax.dot_general(field, jnp.concatenate(high, axis=0), NT, preferred_element_type=F32)
                sums += lax.dot_general(field, jnp.concatenate(low, axis=0), NT, preferred_element_type=F32)
            return sums

        sums = lax.fori_loop(0, width // (BLOCK * UNROLL), block_step, jnp.zeros((24, TILE), F32))
        sums = sums[0:8] + sums[8:16] + sums[16:24]
        pulls = [jnp.sum(pull_ref[k].T, axis=0, keepdims=True) for k in range(3)]
        zero = jnp.zeros((3, TILE), F32)
        sums = jnp.concatenate([sums, *pulls, jnp.zeros((117, TILE), F32)], axis=0).T
        res_ref[rows, :] = sums
        return carry

    lax.fori_loop(0, (total + TILE - 1) // TILE, tile_step, 0)

    def pack(part, carry):
        first = pl.multiple_of(offset_smem[part], 8)
        sums = res_ref[pl.ds(first, slots), :]
        turned = jnp.concatenate([sums, jnp.zeros((128 - slots, 128), F32)], axis=0).T
        own = recv_ref[part]
        result = turned[0:8] - own * turned[6:7]
        send_ref[part] = result - jnp.concatenate([jnp.zeros((3, 128), F32), turned[8:11], jnp.zeros((2, 128), F32)], axis=0)
        return carry

    lax.fori_loop(0, parts, pack, 0, unroll=4)


def finish_kernel(count_ref, recv_ref, accel_ref, jerk_ref):
    parts = recv_ref.shape[0]
    slots = accel_ref.shape[1]

    def add(part, total):
        return total + recv_ref[part]

    total = lax.fori_loop(1, parts, add, recv_ref[0], unroll=8)
    slot = lax.broadcasted_iota(jnp.int32, (8, 128), 1)
    total = jnp.where(slot < count_ref[0], total, 0.0)
    accel_ref[...] = total[0:3, :slots]
    jerk_ref[...] = total[3:6, :slots]


def pair_call(parts, slots, width):
    rows = parts * slots + TILE
    return pl.pallas_call(
        functools.partial(pair_kernel, slots),
        out_shape=jax.ShapeDtypeStruct((parts, 8, 128), F32),
        in_specs=[vmem()] * 4,
        out_specs=vmem(),
        scratch_shapes=[
            pltpu.SMEM((parts, 128), F32),
            pltpu.SMEM((parts,), jnp.int32),
            pltpu.VMEM((rows, 128), F32),
            pltpu.VMEM((3, TILE, 128), F32),
            pltpu.VMEM((3, TILE, 128), F32),
            pltpu.VMEM((rows, 128), F32),
            pltpu.SemaphoreType.DMA,
        ],
        compiler_params=pltpu.CompilerParams(vmem_limit_bytes=48 * 1024 * 1024),
    )


def body(parts, positions, velocities, masses, active_index, active_count):
    slots = active_index.shape[0]
    width = positions.shape[1]
    send, pos, dots, sums = pl.pallas_call(
        functools.partial(prepare_kernel, parts),
        out_shape=(
            jax.ShapeDtypeStruct((parts, 8, 128), F32),
            jax.ShapeDtypeStruct((8, width), F32),
            jax.ShapeDtypeStruct((128, width), BF16),
            jax.ShapeDtypeStruct((24, width), BF16),
        ),
        in_specs=[smem(), smem(), vmem(), vmem(), vmem()],
        out_specs=(vmem(),) * 4,
        scratch_shapes=[pltpu.VMEM((8, width), F32)],
    )(active_index, active_count, positions, velocities, masses.reshape(1, width))
    received = lax.all_to_all(send.reshape(parts * 8, 128), AXES, 0, 0, tiled=True).reshape(parts, 8, 128)
    partial_sums = pair_call(parts, slots, width)(received, pos, dots, sums)
    returned = lax.all_to_all(partial_sums.reshape(parts * 8, 128), AXES, 0, 0, tiled=True).reshape(parts, 8, 128)
    return pl.pallas_call(
        finish_kernel,
        out_shape=(
            jax.ShapeDtypeStruct((3, slots), F32),
            jax.ShapeDtypeStruct((3, slots), F32),
        ),
        in_specs=[smem(), vmem()],
        out_specs=(vmem(), vmem()),
    )(active_count, returned)


def solution(mesh):
    parts = int(np.prod([mesh.shape[axis] for axis in AXES]))
    return jax.shard_map(
        functools.partial(body, parts),
        mesh=mesh,
        in_specs=(P(None, AXES), P(None, AXES), P(AXES), P(AXES), P(AXES)),
        out_specs=(P(None, AXES), P(None, AXES)),
        check_vma=False,
    )
```

time: 61.9 us -> 54.9 us (0.89); the launches traced: 61.6 us -> 55.7 us
  Pallas kernels: 31.8 us -> 26.2 us
  blocking collectives: 23.6 us -> 26.1 us
  other arithmetic: 1.6 us -> 0 us
  local copies, waits for them, and re-layouts: 3.28 us -> 2.13 us
    pallas_call x1, Pallas kernels: 28 us -> 21.9 us  [body(): partial_sums = pair_call(parts, slots, width)(received, pos, dots, sums)]
    all_to_all x2, blocking collectives: 23.6 us -> 26.1 us  [the longest x1 15.5 us: body(): lax.all_to_all(send.reshape(parts * 8, 128), AXES, 0, 0, tiled=True)]
    all_to_all x2 -> x0, other arithmetic: 1.6 us -> none  [the longest x1 0.8 us: body(): returned = lax.all_to_all(partial_sums, AXES, 0, 0)]
    unnamed x6, local copies, waits for them, and re-layouts: 2.77 us -> 2.13 us
where the time goes in v2:
time: 54.9 us; the launch traced here: 55.7 us
  Pallas kernels  26.2 us (48%)
  blocking collectives  26.1 us (48%)
  local copies, waits for them, and re-layouts  2.13 us (4%)
  between operations  1.29 us (2%)
    pallas_call x1, Pallas kernels, body(): partial_sums = pair_call(parts, slots, width)(received, pos, dots, sums)  21.9 us
    all_to_all x1, blocking collectives, body(): lax.all_to_all(send.reshape(parts * 8, 128), AXES, 0, 0, tiled=True)  15.5 us
    all_to_all x1, blocking collectives, body(): lax.all_to_all(partial_sums.reshape(parts * 8, 128), AXES, 0, 0, tiled=True)  10.6 us
    pallas_call x1, Pallas kernels, body(): pl.pallas_call(functools.partial(prepare_kernel, parts), out_shape=(jax.S...  2.74 us
    unnamed x6, local copies, waits for them, and re-layouts  2.13 us
    pallas_call x1, Pallas kernels, body(): pl.pallas_call(finish_kernel, out_shape=(jax.ShapeDtypeStruct((3, slots),...  1.55 us

profile of v2, /device:TPU:0, one launch (start us, length us, event | category | flops | bytes accessed | tf_op | source)
XLA Modules:
  0.0 55.7 jit_solution(15755098022389461827)
XLA Ops:
  1.3 2.7 %shard_map.68 = (f32[32,8,128]{2,1,0:T(8,128)}, f32[8,4096]{1,0:T(8,128)}, bf16[128,4096]{1,0:T(8,128)(2,1)}, bf16[24,4096]{1,0:T(8,128)(2,1)}) custom-call(s32[64]{0:T(128)} %index_ref.1, s32[1]{0:T(128)S(6)} %copy.7.count_ref, f32[3,4096]{1,0:T(4,128)} %pos_ref.1, f32[3,4096]{1,0:T(4,128)} %vel_ref.1, f32[1,4096]{1,0:T(1,128)} %bitcast.1), custom_call_target="tpu_custom_call" | custom-call | tf_op jit(solution)/shard_map/pallas_call | solution.py:198
  4.0 0.0 copy-start.1
  4.0 15.5 %all_to_all.12.recv_ref = f32[32,8,128]{2,1,0:T(8,128)S(1)} all-to-all(f32[32,8,128]{2,1,0:T(8,128)} %get-tuple-element.6), channel_id=1, replica_groups=mesh['col'=8,'row'=4] {'col','row'}, dimensions={0} | all-to-all | bytes 262144 | tf_op jit(solution)/shard_map/all_to_all | solution.py:210
  19.6 0.0 copy-done.1
  19.6 0.0 copy-start
  19.6 1.2 %copy-done = bf16[128,4096]{1,0:T(8,128)(2,1)S(1)} copy-done((bf16[128,4096]{1,0:T(8,128)(2,1)S(1)}, bf16[128,4096]{1,0:T(8,128)(2,1)}, u32[]{:S(2)}) %copy-start) | copy-done | bytes 1048600
  20.8 0.0 copy-start.2
  20.8 0.9 %copy-done.2 = f32[8,4096]{1,0:T(8,128)S(1)} copy-done((f32[8,4096]{1,0:T(8,128)S(1)}, f32[8,4096]{1,0:T(8,128)}, u32[]{:S(2)}) %copy-start.2) | copy-done | bytes 131096
  21.7 21.9 %shard_map.69 = f32[32,8,128]{2,1,0:T(8,128)S(1)} custom-call(f32[32,8,128]{2,1,0:T(8,128)S(1)} %all_to_all.12.recv_ref, f32[8,4096]{1,0:T(8,128)S(1)} %copy-done.2, bf16[128,4096]{1,0:T(8,128)(2,1)S(1)} %copy-done, bf16[24,4096]{1,0:T(8,128)(2,1)S(1)} %copy-done.1), custom_call_target="tpu_custom_call" | custom-call | tf_op jit(solution)/shard_map/pallas_call | solution.py:211
  43.6 10.6 %all_to_all.13.recv_ref = f32[32,8,128]{2,1,0:T(8,128)} all-to-all(f32[32,8,128]{2,1,0:T(8,128)S(1)} %shard_map.69), channel_id=1, replica_groups=mesh['col'=8,'row'=4] {'col','row'}, dimensions={0} | all-to-all | bytes 262144 | tf_op jit(solution)/shard_map/all_to_all | solution.py:212
  54.2 1.5 %shard_map.70 = (f32[3,64]{1,0:T(4,128)}, f32[3,64]{1,0:T(4,128)}) custom-call(s32[1]{0:T(128)S(6)} %copy.7.count_ref, f32[32,8,128]{2,1,0:T(8,128)} %all_to_all.13.recv_ref), custom_call_target="tpu_custom_call" | custom-call | tf_op jit(solution)/shard_map/pallas_call | solution.py:213
Async XLA Ops:
  4.0 15.5 %copy-start.1 = (bf16[24,4096]{1,0:T(8,128)(2,1)S(1)}, bf16[24,4096]{1,0:T(8,128)(2,1)}, u32[]{:S(2)}) copy-start(bf16[24,4096]{1,0:T(8,128)(2,1)} %get-tuple-element.9.sum_ref) | copy-start | bytes 589828
  19.6 1.2 %copy-start = (bf16[128,4096]{1,0:T(8,128)(2,1)S(1)}, bf16[128,4096]{1,0:T(8,128)(2,1)}, u32[]{:S(2)}) copy-start(bf16[128,4096]{1,0:T(8,128)(2,1)} %get-tuple-element.8.dot_ref) | copy-start | bytes 3145732
  20.8 0.9 %copy-start.2 = (f32[8,4096]{1,0:T(8,128)S(1)}, f32[8,4096]{1,0:T(8,128)}, u32[]{:S(2)}) copy-start(f32[8,4096]{1,0:T(8,128)} %get-tuple-element.7.pos_ref) | copy-start | bytes 393220

commit v3 on v2

v3 whole, which is shorter than its diff:
```python
import functools

import jax
import jax.numpy as jnp
import numpy as np
from jax import lax
from jax.experimental import pallas as pl
from jax.experimental.pallas import tpu as pltpu
from jax.sharding import PartitionSpec as P

AXES = ("col", "row")
SOFTEN = 0.0001
F32 = jnp.float32
BF16 = jnp.bfloat16
TILE = 128
CH = 16
BLOCK = 256
UNROLL = 16
PAIRS = ((0, 0), (1, 0), (0, 1), (1, 1), (2, 0), (0, 2))
RAW = 8 * len(PAIRS)
DEPTH = 64
NN = (((1,), (0,)), ((), ()))
NT = (((1,), (1,)), ((), ()))


def vmem():
    return pl.BlockSpec(memory_space=pltpu.VMEM)


def smem():
    return pl.BlockSpec(memory_space=pltpu.SMEM)


def pieces(value):
    first = value.astype(BF16).astype(F32)
    rest = value - first
    second = rest.astype(BF16).astype(F32)
    return first, second, (rest - second).astype(BF16).astype(F32)


def prepare_kernel(parts, index_ref, count_ref, pos_ref, vel_ref, send_ref, stars_ref):
    slots = index_ref.shape[0]
    pos, vel = pos_ref[...], vel_ref[...]
    cross = jnp.sum(pos * vel, axis=0, keepdims=True)
    stars_ref[...] = jnp.concatenate([pos, cross, vel, cross], axis=0)
    lane = lax.broadcasted_iota(jnp.int32, (8, 128), 1)
    picked = jnp.zeros((8, 128), F32)
    for slot in range(slots):
        star = index_ref[slot]
        tile = stars_ref[:, pl.ds(pl.multiple_of((star // 128) * 128, 128), 128)]
        moved = pltpu.roll(tile, (slot - star % 128) % 128, 1)
        picked = jnp.where(lane == slot, moved, picked)
    row = lax.broadcasted_iota(jnp.int32, (4, 128), 0)
    upper = jnp.where(row == 3, count_ref[0].astype(F32), pltpu.roll(picked[4:8], slots, 1))
    payload = jnp.where(lane[0:4] < slots, picked[0:4], upper)

    def fill(part, carry):
        send_ref[part] = payload
        return carry

    lax.fori_loop(0, parts, fill, 0, unroll=8)


def pair_kernel(slots, recv_ref, pos_ref, vel_ref, mass_ref, send_ref, count_smem, offset_smem, dot_ref, sum_ref, slot_ref, own_ref, pull_ref, res_ref, sem):
    parts = recv_ref.shape[0]
    width = pos_ref.shape[1]
    copy = pltpu.make_async_copy(recv_ref.at[:, 3], count_smem, sem)
    copy.start()

    def star_step(step, carry):
        cols = pl.ds(pl.multiple_of(step * 512, 512), 512)
        pos, vel, mass = pos_ref[:, cols], vel_ref[:, cols], mass_ref[:, cols]
        heavy = 3.0 * mass
        cross = jnp.sum(pos * vel, axis=0, keepdims=True)
        dots = pieces(jnp.concatenate([-heavy * vel, heavy, -heavy * pos, heavy * cross], axis=0))
        for k, (mine, _) in enumerate(PAIRS):
            dot_ref[8 * k : 8 * k + 8, cols] = dots[mine].astype(BF16)
        dot_ref[RAW:DEPTH, cols] = jnp.zeros((DEPTH - RAW, 512), BF16)
        sums = pieces(jnp.concatenate([mass * pos, mass, mass * vel, jnp.zeros_like(mass)], axis=0))
        for k in range(3):
            sum_ref[8 * k : 8 * k + 8, cols] = sums[k].astype(BF16)
        return carry

    lax.fori_loop(0, width // 512, star_step, 0)
    copy.wait()

    lane = lax.broadcasted_iota(jnp.int32, (8, 128), 1)
    row = lax.broadcasted_iota(jnp.int32, (8, 128), 0)

    def gather(part, total):
        offset_smem[part] = total
        raw = recv_ref[part]
        own = jnp.concatenate([raw, pltpu.roll(raw, 128 - slots, 1)], axis=0)
        own = jnp.where(row == 7, 1.0, own)
        tile, start = total // 128, total % 128
        moved = pltpu.roll(own, start, 1)
        slot_ref[tile] = jnp.where(lane < start, slot_ref[tile], moved)
        slot_ref[tile + 1] = moved
        return total + count_smem[part, 127].astype(jnp.int32)

    total = lax.fori_loop(0, parts, gather, 0, unroll=8)

    def tile_step(tile, carry):
        slot = slot_ref[tile]
        split = pieces(slot)
        rows = [split[theirs] for _, theirs in PAIRS] + [slot, jnp.zeros((DEPTH - RAW - 8, TILE), F32)]
        act = jnp.concatenate(rows, axis=0).T
        for k in range(3):
            own_ref[k] = jnp.broadcast_to(act[:, RAW + k : RAW + k + 1], (TILE, 128))
            pull_ref[k] = jnp.zeros((TILE, 128), F32)
        left = act.astype(BF16)

        def block_step(step, sums):
            for block in range(UNROLL):
                cols = pl.ds(pl.multiple_of((step * UNROLL + block) * BLOCK, BLOCK), BLOCK)
                dot = lax.dot_general(left, dot_ref[:, cols], NN, preferred_element_type=F32)
                high, low = [], []
                for chunk in range(TILE // CH):
                    part = slice(chunk * CH, chunk * CH + CH)
                    own = [own_ref[k, part, :] for k in range(3)]
                    acc = [pull_ref[k, part, :] for k in range(3)]
                    highs, lows = [], []
                    for half in range(BLOCK // 128):
                        lanes = pl.ds(pl.multiple_of((step * UNROLL + block) * BLOCK + half * 128, 128), 128)
                        star = [jnp.broadcast_to(pos_ref[k : k + 1, lanes], (CH, 128)) for k in range(3)]
                        dx = [star[k] - own[k] for k in range(3)]
                        squared = dx[2] * dx[2] + (dx[1] * dx[1] + (dx[0] * dx[0] + SOFTEN))
                        root = lax.rsqrt(squared)
                        inverse = root * root
                        cube = root * inverse
                        pull = (dot[part, half * 128 : half * 128 + 128] * inverse) * cube
                        for k in range(3):
                            acc[k] += pull * dx[k]
                        first = cube.astype(BF16)
                        highs.append(first)
                        lows.append((cube - first.astype(F32)).astype(BF16))
                    for k in range(3):
                        pull_ref[k, part, :] = acc[k]
                    high.append(jnp.concatenate(highs, axis=1))
                    low.append(jnp.concatenate(lows, axis=1))
                field = sum_ref[:, cols]
                sums += lax.dot_general(field, jnp.concatenate(high, axis=0), NT, preferred_element_type=F32)
                sums += lax.dot_general(field, jnp.concatenate(low, axis=0), NT, preferred_element_type=F32)
            return sums

        sums = lax.fori_loop(0, width // (BLOCK * UNROLL), block_step, jnp.zeros((24, TILE), F32))
        sums = sums[0:8] + sums[8:16] + sums[16:24]
        pulls = [jnp.sum(pull_ref[k].T, axis=0, keepdims=True) for k in range(3)]
        pulls = jnp.concatenate([jnp.zeros((4, TILE), F32), *pulls, jnp.zeros((1, TILE), F32)], axis=0)
        res_ref[tile] = sums - slot * sums[3:4] - pulls
        return carry

    lax.fori_loop(0, (total + TILE - 1) // TILE, tile_step, 0)

    def spread(part, carry):
        first = offset_smem[part]
        tile, start = first // 128, first % 128
        back = (128 - start) % 128
        moved = jnp.where(lane < 128 - start, pltpu.roll(res_ref[tile], back, 1), pltpu.roll(res_ref[tile + 1], back, 1))
        send_ref[part] = jnp.where(lane[0:4] < slots, moved[0:4], pltpu.roll(moved[4:8], slots, 1))
        return carry

    lax.fori_loop(0, parts, spread, 0, unroll=8)


def finish_kernel(count_ref, recv_ref, accel_ref, jerk_ref):
    parts = recv_ref.shape[0]
    slots = accel_ref.shape[1]

    def add(part, total):
        return total + recv_ref[part]

    total = lax.fori_loop(1, parts, add, recv_ref[0], unroll=8)
    lane = lax.broadcasted_iota(jnp.int32, (4, 128), 1)
    total = jnp.where(lane % slots < count_ref[0], total, 0.0)
    accel_ref[...] = total[0:3, :slots]
    jerk_ref[...] = total[0:3, slots : 2 * slots]


def pair_call(parts, slots, width):
    tiles = (parts * slots) // TILE + 2
    return pl.pallas_call(
        functools.partial(pair_kernel, slots),
        out_shape=jax.ShapeDtypeStruct((parts, 4, 128), F32),
        in_specs=[vmem()] * 4,
        out_specs=vmem(),
        scratch_shapes=[
            pltpu.SMEM((parts, 128), F32),
            pltpu.SMEM((parts,), jnp.int32),
            pltpu.VMEM((DEPTH, width), BF16),
            pltpu.VMEM((24, width), BF16),
            pltpu.VMEM((tiles, 8, 128), F32),
            pltpu.VMEM((3, TILE, 128), F32),
            pltpu.VMEM((3, TILE, 128), F32),
            pltpu.VMEM((tiles, 8, 128), F32),
            pltpu.SemaphoreType.DMA,
        ],
        compiler_params=pltpu.CompilerParams(vmem_limit_bytes=48 * 1024 * 1024),
    )


def body(parts, positions, velocities, masses, active_index, active_count):
    slots = active_index.shape[0]
    width = positions.shape[1]
    send = pl.pallas_call(
        functools.partial(prepare_kernel, parts),
        out_shape=jax.ShapeDtypeStruct((parts, 4, 128), F32),
        in_specs=[smem(), smem(), vmem(), vmem()],
        out_specs=vmem(),
        scratch_shapes=[pltpu.VMEM((8, width), F32)],
    )(active_index, active_count, positions, velocities)
    received = lax.all_to_all(send, AXES, 0, 0, tiled=True)
    partial_sums = pair_call(parts, slots, width)(received, positions, velocities, masses.reshape(1, width))
    returned = lax.all_to_all(partial_sums, AXES, 0, 0, tiled=True)
    return pl.pallas_call(
        finish_kernel,
        out_shape=(
            jax.ShapeDtypeStruct((3, slots), F32),
            jax.ShapeDtypeStruct((3, slots), F32),
        ),
        in_specs=[smem(), vmem()],
        out_specs=(vmem(), vmem()),
    )(active_count, returned)


def solution(mesh):
    parts = int(np.prod([mesh.shape[axis] for axis in AXES]))
    return jax.shard_map(
        functools.partial(body, parts),
        mesh=mesh,
        in_specs=(P(None, AXES), P(None, AXES), P(AXES), P(AXES), P(AXES)),
        out_specs=(P(None, AXES), P(None, AXES)),
        check_vma=False,
    )
```

time: 54.9 us -> 46 us (0.84)
  Pallas kernels: 26.2 us -> 21 us
  local copies, waits for them, and re-layouts: 2.13 us -> 0.01 us
  blocking collectives: 26.1 us -> 24.5 us
    pallas_call x2, Pallas kernels: 24.6 us -> 19.4 us  [the longest x1 17.2 us: body(): pair_call(parts, slots, width)]
    unnamed x6, local copies, waits for them, and re-layouts: 2.13 us -> 0.01 us
    all_to_all x2, blocking collectives: 26.1 us -> 24.5 us  [the longest x1 14.7 us: body(): received = lax.all_to_all(send, AXES, 0, 0, tiled=True)]
where the time goes in v3:
time: 46 us; the launch traced here: 46.8 us
  blocking collectives  24.5 us (53%)
  Pallas kernels  21 us (46%)
  between operations  1.3 us (3%)
    pallas_call x1, Pallas kernels, body(): pair_call(parts, slots, width)  17.2 us
    all_to_all x1, blocking collectives, body(): received = lax.all_to_all(send, AXES, 0, 0, tiled=True)  14.7 us
    all_to_all x1, blocking collectives, body(): returned = lax.all_to_all(partial_sums, AXES, 0, 0, tiled=True)  9.78 us
    pallas_call x1, Pallas kernels, body(): pl.pallas_call(functools.partial(prepare_kernel, parts), out_shape=jax.Sh...  2.25 us
    pallas_call x1, Pallas kernels, body(): pl.pallas_call(finish_kernel, out_shape=(jax.ShapeDtypeStruct((3, slots),...  1.55 us

profile of v3, /device:TPU:0, one launch (start us, length us, event | category | flops | bytes accessed | tf_op | source)
XLA Modules:
  0.0 46.8 jit_solution(15500749383415776247)
XLA Ops:
  1.3 0.0 copy-start.2
  1.3 2.2 %shard_map.68 = f32[32,4,128]{2,1,0:T(4,128)} custom-call(s32[64]{0:T(128)} %index_ref.1, s32[1]{0:T(128)S(6)} %copy.7.count_ref, f32[3,4096]{1,0:T(4,128)} %pos_ref.3, f32[3,4096]{1,0:T(4,128)} %vel_ref.3), custom_call_target="tpu_custom_call" | custom-call | tf_op jit(solution)/shard_map/pallas_call | solution.py:205
  3.5 0.0 copy-start
  3.5 0.0 copy-start.1
  3.5 14.7 %all_to_all.10.recv_ref = f32[32,4,128]{2,1,0:T(4,128)S(1)} all-to-all(f32[32,4,128]{2,1,0:T(4,128)} %shard_map.68), channel_id=1, replica_groups=mesh['col'=8,'row'=4] {'col','row'}, dimensions={0} | all-to-all | bytes 131072 | tf_op jit(solution)/shard_map/all_to_all | solution.py:212
  18.3 0.0 copy-done.2
  18.3 0.0 copy-done
  18.3 0.0 copy-done.1
  18.3 17.2 %shard_map.69 = f32[32,4,128]{2,1,0:T(4,128)S(1)} custom-call(f32[32,4,128]{2,1,0:T(4,128)S(1)} %all_to_all.10.recv_ref, f32[3,4096]{1,0:T(4,128)S(1)} %copy-done, f32[3,4096]{1,0:T(4,128)S(1)} %copy-done.1, f32[1,4096]{1,0:T(1,128)S(1)} %bitcast.1), custom_call_target="tpu_custom_call" | custom-call | tf_op jit(solution)/shard_map/pallas_call | solution.py:213
  35.5 9.8 %all_to_all.11.recv_ref = f32[32,4,128]{2,1,0:T(4,128)} all-to-all(f32[32,4,128]{2,1,0:T(4,128)S(1)} %shard_map.69), channel_id=1, replica_groups=mesh['col'=8,'row'=4] {'col','row'}, dimensions={0} | all-to-all | bytes 131072 | tf_op jit(solution)/shard_map/all_to_all | solution.py:214
  45.3 1.5 %shard_map.70 = (f32[3,64]{1,0:T(4,128)}, f32[3,64]{1,0:T(4,128)}) custom-call(s32[1]{0:T(128)S(6)} %copy.7.count_ref, f32[32,4,128]{2,1,0:T(4,128)} %all_to_all.11.recv_ref), custom_call_target="tpu_custom_call" | custom-call | tf_op jit(solution)/shard_map/pallas_call | solution.py:215
Async XLA Ops:
  1.3 17.0 %copy-start.2 = (f32[4096]{0:T(1024)S(1)}, f32[4096]{0:T(1024)}, u32[]{:S(2)}) copy-start(f32[4096]{0:T(1024)} %param.7) | copy-start | bytes 49156
  3.5 14.7 %copy-start = (f32[3,4096]{1,0:T(4,128)S(1)}, f32[3,4096]{1,0:T(4,128)}, u32[]{:S(2)}) copy-start(f32[3,4096]{1,0:T(4,128)} %pos_ref.3) | copy-start | bytes 147460
  3.5 14.7 %copy-start.1 = (f32[3,4096]{1,0:T(4,128)S(1)}, f32[3,4096]{1,0:T(4,128)}, u32[]{:S(2)}) copy-start(f32[3,4096]{1,0:T(4,128)} %vel_ref.3) | copy-start | bytes 147460

commit v4 on v3

--- a/solution.py
+++ b/solution.py
@@ -10,6 +10,7 @@
 
 AXES = ("col", "row")
 SOFTEN = 0.0001
+MARK = 8.0
 F32 = jnp.float32
 BF16 = jnp.bfloat16
 TILE = 128
@@ -31,6 +32,10 @@
     return pl.BlockSpec(memory_space=pltpu.SMEM)
 
 
+def hbm():
+    return pl.BlockSpec(memory_space=pltpu.HBM)
+
+
 def pieces(value):
     first = value.astype(BF16).astype(F32)
     rest = value - first
@@ -38,24 +43,34 @@
     return first, second, (rest - second).astype(BF16).astype(F32)
 
 
-def prepare_kernel(parts, index_ref, count_ref, pos_ref, vel_ref, send_ref, stars_ref):
+def prepare_kernel(parts, index_ref, count_ref, pos_hbm, vel_hbm, send_ref, pos_ref, vel_ref, sems):
     slots = index_ref.shape[0]
-    pos, vel = pos_ref[...], vel_ref[...]
-    cross = jnp.sum(pos * vel, axis=0, keepdims=True)
-    stars_ref[...] = jnp.concatenate([pos, cross, vel, cross], axis=0)
-    lane = lax.broadcasted_iota(jnp.int32, (8, 128), 1)
-    picked = jnp.zeros((8, 128), F32)
+    copies = [
+        pltpu.make_async_copy(pos_hbm, pos_ref, sems.at[0]),
+        pltpu.make_async_copy(vel_hbm, vel_ref, sems.at[1]),
+    ]
+    for copy in copies:
+        copy.start()
+    for copy in copies:
+        copy.wait()
+    lane = lax.broadcasted_iota(jnp.int32, (3, 128), 1)
+    picked = jnp.zeros((3, 128), F32)
     for slot in range(slots):
         star = index_ref[slot]
-        tile = stars_ref[:, pl.ds(pl.multiple_of((star // 128) * 128, 128), 128)]
-        moved = pltpu.roll(tile, (slot - star % 128) % 128, 1)
+        tile = pl.ds(pl.multiple_of((star >> 7) << 7, 128), 128)
+        shift = slot - star
+        moved = pltpu.roll(pos_ref[:, tile], shift & 127, 1)
         picked = jnp.where(lane == slot, moved, picked)
-    row = lax.broadcasted_iota(jnp.int32, (4, 128), 0)
-    upper = jnp.where(row == 3, count_ref[0].astype(F32), pltpu.roll(picked[4:8], slots, 1))
-    payload = jnp.where(lane[0:4] < slots, picked[0:4], upper)
+        moved = pltpu.roll(vel_ref[:, tile], (shift + slots) & 127, 1)
+        picked = jnp.where(lane == slot + slots, moved, picked)
+    row = lax.broadcasted_iota(jnp.int32, (3, 128), 0)
+    count = count_ref[0]
+    mark = (row == 0) & (lane == slots - 1) & (count < slots)
+    picked = jnp.where(mark, MARK + count.astype(F32), picked)
 
     def fill(part, carry):
-        send_ref[part] = payload
+        for k in range(3):
+            send_ref[part, :, 128 * k : 128 * k + 128] = picked[k : k + 1]
         return carry
 
     lax.fori_loop(0, parts, fill, 0, unroll=8)
@@ -64,7 +79,7 @@
 def pair_kernel(slots, recv_ref, pos_ref, vel_ref, mass_ref, send_ref, count_smem, offset_smem, dot_ref, sum_ref, slot_ref, own_ref, pull_ref, res_ref, sem):
     parts = recv_ref.shape[0]
     width = pos_ref.shape[1]
-    copy = pltpu.make_async_copy(recv_ref.at[:, 3], count_smem, sem)
+    copy = pltpu.make_async_copy(recv_ref.at[:, 0, 0:128], count_smem, sem)
     copy.start()
 
     def star_step(step, carry):
@@ -89,19 +104,22 @@
 
     def gather(part, total):
         offset_smem[part] = total
-        raw = recv_ref[part]
+        raw = [recv_ref[part, :, 128 * k : 128 * k + 128] for k in range(3)]
+        raw = jnp.concatenate([*raw, raw[0]], axis=0)
         own = jnp.concatenate([raw, pltpu.roll(raw, 128 - slots, 1)], axis=0)
-        own = jnp.where(row == 7, 1.0, own)
-        tile, start = total // 128, total % 128
+        tile, start = total >> 7, total & 127
         moved = pltpu.roll(own, start, 1)
         slot_ref[tile] = jnp.where(lane < start, slot_ref[tile], moved)
         slot_ref[tile + 1] = moved
-        return total + count_smem[part, 127].astype(jnp.int32)
+        last = count_smem[part, slots - 1]
+        return total + jnp.where(last < MARK, slots, (last - MARK).astype(jnp.int32))
 
     total = lax.fori_loop(0, parts, gather, 0, unroll=8)
 
     def tile_step(tile, carry):
         slot = slot_ref[tile]
+        cross = jnp.sum(slot[0:3] * slot[4:7], axis=0, keepdims=True)
+        slot = jnp.where(row == 7, 1.0, jnp.where(row == 3, cross, slot))
         split = pieces(slot)
         rows = [split[theirs] for _, theirs in PAIRS] + [slot, jnp.zeros((DEPTH - RAW - 8, TILE), F32)]
         act = jnp.concatenate(rows, axis=0).T
@@ -139,11 +157,11 @@
                     high.append(jnp.concatenate(highs, axis=1))
                     low.append(jnp.concatenate(lows, axis=1))
                 field = sum_ref[:, cols]
-                sums += lax.dot_general(field, jnp.concatenate(high, axis=0), NT, preferred_element_type=F32)
-                sums += lax.dot_general(field, jnp.concatenate(low, axis=0), NT, preferred_element_type=F32)
+                sums += lax.dot_general(field, jnp.concatenate(high + low, axis=0), NT, preferred_element_type=F32)
             return sums
 
-        sums = lax.fori_loop(0, width // (BLOCK * UNROLL), block_step, jnp.zeros((24, TILE), F32))
+        sums = lax.fori_loop(0, width // (BLOCK * UNROLL), block_step, jnp.zeros((24, 2 * TILE), F32))
+        sums = sums[:, :TILE] + sums[:, TILE:]
         sums = sums[0:8] + sums[8:16] + sums[16:24]
         pulls = [jnp.sum(pull_ref[k].T, axis=0, keepdims=True) for k in range(3)]
         pulls = jnp.concatenate([jnp.zeros((4, TILE), F32), *pulls, jnp.zeros((1, TILE), F32)], axis=0)
@@ -154,34 +172,33 @@
 
     def spread(part, carry):
         first = offset_smem[part]
-        tile, start = first // 128, first % 128
-        back = (128 - start) % 128
+        tile, start = first >> 7, first & 127
+        back = (128 - start) & 127
         moved = jnp.where(lane < 128 - start, pltpu.roll(res_ref[tile], back, 1), pltpu.roll(res_ref[tile + 1], back, 1))
-        send_ref[part] = jnp.where(lane[0:4] < slots, moved[0:4], pltpu.roll(moved[4:8], slots, 1))
+        moved = jnp.where(lane[0:4] < slots, moved[0:4], pltpu.roll(moved[4:8], slots, 1))
+        for k in range(3):
+            send_ref[part, :, 128 * k : 128 * k + 128] = moved[k : k + 1]
         return carry
 
     lax.fori_loop(0, parts, spread, 0, unroll=8)
 
 
 def finish_kernel(count_ref, recv_ref, accel_ref, jerk_ref):
-    parts = recv_ref.shape[0]
     slots = accel_ref.shape[1]
-
-    def add(part, total):
-        return total + recv_ref[part]
-
-    total = lax.fori_loop(1, parts, add, recv_ref[0], unroll=8)
-    lane = lax.broadcasted_iota(jnp.int32, (4, 128), 1)
-    total = jnp.where(lane % slots < count_ref[0], total, 0.0)
-    accel_ref[...] = total[0:3, :slots]
-    jerk_ref[...] = total[0:3, slots : 2 * slots]
+    total = jnp.sum(recv_ref[...], axis=0)
+    for k in range(3):
+        row = total[:, 128 * k : 128 * k + 128]
+        lane = lax.broadcasted_iota(jnp.int32, row.shape, 1)
+        row = jnp.where(lane % slots < count_ref[0], row, 0.0)
+        accel_ref[k : k + 1, :] = row[:, :slots]
+        jerk_ref[k : k + 1, :] = row[:, slots : 2 * slots]
 
 
 def pair_call(parts, slots, width):
     tiles = (parts * slots) // TILE + 2
     return pl.pallas_call(
         functools.partial(pair_kernel, slots),
-        out_shape=jax.ShapeDtypeStruct((parts, 4, 128), F32),
+        out_shape=jax.ShapeDtypeStruct((parts, 1, 384), F32),
         in_specs=[vmem()] * 4,
         out_specs=vmem(),
         scratch_shapes=[
@@ -204,10 +221,15 @@
     width = positions.shape[1]
     send = pl.pallas_call(
         functools.partial(prepare_kernel, parts),
-        out_shape=jax.ShapeDtypeStruct((parts, 4, 128), F32),
-        in_specs=[smem(), smem(), vmem(), vmem()],
+        out_shape=jax.ShapeDtypeStruct((parts, 1, 384), F32),
+        in_specs=[smem(), smem(), hbm(), hbm()],
         out_specs=vmem(),
-        scratch_shapes=[pltpu.VMEM((8, width), F32)],
+        scratch_shapes=[
+            pltpu.VMEM((3, width), F32),
+            pltpu.VMEM((3, width), F32),
+            pltpu.SemaphoreType.DMA((2,)),
+        ],
+        compiler_params=pltpu.CompilerParams(vmem_limit_bytes=16 * 1024 * 1024),
     )(active_index, active_count, positions, velocities)
     received = lax.all_to_all(send, AXES, 0, 0, tiled=True)
     partial_sums = pair_call(parts, slots, width)(received, positions, velocities, masses.reshape(1, width))
@@ -220,6 +242,7 @@
         ),
         in_specs=[smem(), vmem()],
         out_specs=(vmem(), vmem()),
+        compiler_params=pltpu.CompilerParams(vmem_limit_bytes=16 * 1024 * 1024),
     )(active_count, returned)
 
 

time: 46 us -> 45.1 us (0.980); the launches traced: 46.8 us -> 44.8 us
  Pallas kernels: 21 us -> 18.3 us
  local copies, waits for them, and re-layouts: 0.01 us -> 1.69 us
  blocking collectives: 24.5 us -> 23.5 us
    unnamed x6 -> x12, local copies, waits for them, and re-layouts: 0.01 us -> 1.69 us
    pallas_call x1, Pallas kernels: 2.25 us -> 1.03 us  [body(): pl.pallas_call(functools.partial(prepare_kernel, parts), out_shape=jax.Sh...]
    pallas_call x1, Pallas kernels: 1.55 us -> 0.7 us  [body(): pl.pallas_call(finish_kernel, out_shape=(jax.ShapeDtypeStruct((3, slots),...]
    all_to_all x1, blocking collectives: 9.78 us -> 9.03 us  [body(): returned = lax.all_to_all(partial_sums, AXES, 0, 0, tiled=True)]
    pallas_call x1, Pallas kernels: 17.2 us -> 16.5 us  [body(): pair_call(parts, slots, width)]
where the time goes in v4:
time: 45.1 us; the launch traced here: 44.8 us
  blocking collectives  23.5 us (52%)
  Pallas kernels  18.3 us (41%)
  local copies, waits for them, and re-layouts  1.69 us (4%)
  between operations  1.35 us (3%)
    pallas_call x1, Pallas kernels, body(): pair_call(parts, slots, width)  16.5 us
    all_to_all x1, blocking collectives, body(): received = lax.all_to_all(send, AXES, 0, 0, tiled=True)  14.4 us
    all_to_all x1, blocking collectives, body(): returned = lax.all_to_all(partial_sums, AXES, 0, 0, tiled=True)  9.03 us
    unnamed x12, local copies, waits for them, and re-layouts  1.69 us
    pallas_call x1, Pallas kernels, body(): pl.pallas_call(functools.partial(prepare_kernel, parts), out_shape=jax.Sh...  1.03 us

profile of v4, /device:TPU:0, one launch (start us, length us, event | category | flops | bytes accessed | tf_op | source)
XLA Modules:
  0.0 44.8 jit_solution(13568575562427910812)
XLA Ops:
  0.6 0.0 copy-start.5
  1.3 0.0 copy-done.5
  1.3 0.0 copy-start
  1.3 0.8 %copy-done = f32[3,4096]{1,0:T(4,128)S(1)} copy-done((f32[3,4096]{1,0:T(4,128)S(1)}, f32[3,4096]{1,0:T(4,128)}, u32[]{:S(2)}) %copy-start) | copy-done | bytes 49176
  2.2 0.0 copy-start.2
  2.2 0.8 %copy-done.2 = f32[3,4096]{1,0:T(4,128)S(1)} copy-done((f32[3,4096]{1,0:T(4,128)S(1)}, f32[3,4096]{1,0:T(4,128)}, u32[]{:S(2)}) %copy-start.2) | copy-done | bytes 49176
  3.0 0.0 copy-start.3
  3.0 1.0 %shard_map.68 = f32[32,1,384]{2,1,0:T(1,128)S(1)} custom-call(s32[64]{0:T(128)S(1)} %copy-done.5, s32[1]{0:T(128)S(6)} %copy.7.count_ref, f32[3,4096]{1,0:T(4,128)S(1)} %copy-done, f32[3,4096]{1,0:T(4,128)S(1)} %copy-done.2), custom_call_target="tpu_custom_call" | custom-call | tf_op jit(solution)/shard_map/pallas_call | solution.py:222
  4.0 0.0 copy-start.1
  4.0 0.0 copy-start.4
  4.1 14.4 %all_to_all.10.recv_ref = f32[32,1,384]{2,1,0:T(1,128)S(1)} all-to-all(f32[32,1,384]{2,1,0:T(1,128)S(1)} %shard_map.68), channel_id=1, replica_groups=mesh['col'=8,'row'=4] {'col','row'}, dimensions={0} | all-to-all | bytes 98304 | tf_op jit(solution)/shard_map/all_to_all | solution.py:234
  18.5 0.0 copy-done.3
  18.5 0.0 copy-done.1
  18.5 0.0 copy-done.4
  18.5 16.5 %shard_map.69 = f32[32,1,384]{2,1,0:T(1,128)S(1)} custom-call(f32[32,1,384]{2,1,0:T(1,128)S(1)} %all_to_all.10.recv_ref, f32[3,4096]{1,0:T(4,128)S(1)} %copy-done.1, f32[3,4096]{1,0:T(4,128)S(1)} %copy-done.3, f32[1,4096]{1,0:T(1,128)S(1)} %bitcast.1), custom_call_target="tpu_custom_call" | custom-call | tf_op jit(solution)/shard_map/pallas_call | solution.py:235
  35.1 9.0 %all_to_all.11.recv_ref = f32[32,1,384]{2,1,0:T(1,128)S(1)} all-to-all(f32[32,1,384]{2,1,0:T(1,128)S(1)} %shard_map.69), channel_id=1, replica_groups=mesh['col'=8,'row'=4] {'col','row'}, dimensions={0} | all-to-all | bytes 98304 | tf_op jit(solution)/shard_map/all_to_all | solution.py:236
  44.1 0.7 %shard_map.70 = (f32[3,64]{1,0:T(4,128)}, f32[3,64]{1,0:T(4,128)}) custom-call(s32[1]{0:T(128)S(6)} %copy.7.count_ref, f32[32,1,384]{2,1,0:T(1,128)S(1)} %all_to_all.11.recv_ref), custom_call_target="tpu_custom_call" | custom-call | tf_op jit(solution)/shard_map/pallas_call | solution.py:237
Async XLA Ops:
  0.6 0.7 %copy-start.5 = (s32[64]{0:T(128)S(1)}, s32[64]{0:T(128)}, u32[]{:S(2)}) copy-start(s32[64]{0:T(128)} %index_ref.1) | copy-start | bytes 772
  1.3 0.8 %copy-start = (f32[3,4096]{1,0:T(4,128)S(1)}, f32[3,4096]{1,0:T(4,128)}, u32[]{:S(2)}) copy-start(f32[3,4096]{1,0:T(4,128)} %pos_ref.1) | copy-start | bytes 147460
  2.2 0.8 %copy-start.2 = (f32[3,4096]{1,0:T(4,128)S(1)}, f32[3,4096]{1,0:T(4,128)}, u32[]{:S(2)}) copy-start(f32[3,4096]{1,0:T(4,128)} %vel_ref.1) | copy-start | bytes 147460
  3.0 15.5 %copy-start.3 = (f32[3,4096]{1,0:T(4,128)S(1)}, f32[3,4096]{1,0:T(4,128)}, u32[]{:S(2)}) copy-start(f32[3,4096]{1,0:T(4,128)} %vel_ref.1) | copy-start | bytes 147460
  4.0 14.5 %copy-start.1 = (f32[3,4096]{1,0:T(4,128)S(1)}, f32[3,4096]{1,0:T(4,128)}, u32[]{:S(2)}) copy-start(f32[3,4096]{1,0:T(4,128)} %pos_ref.1) | copy-start | bytes 147460
  4.0 14.5 %copy-start.4 = (f32[4096]{0:T(1024)S(1)}, f32[4096]{0:T(1024)}, u32[]{:S(2)}) copy-start(f32[4096]{0:T(1024)} %param.7) | copy-start | bytes 49156
